TPU v7x, 32 devices: a whole 2x2x4 slice. The times are simulated.
32 devices in a mesh: freq: 2 (over y), harm: 4 (over z), wall: 4 (over x, core).
Axes of the slice: x: 2, y: 2, z: 4, core: 2. Of those that a mesh axis runs over, the one named last changes fastest.
Arguments:
- sketch: bfloat16 [32, 1024, 128], P(('freq', 'harm'), 'wall'), parts along dimension 0, may hold values from -48 to 48
- inverse_blocks: bfloat16 [32, 1024, 1024], P(('freq', 'harm'), 'wall'), parts along dimension 0, may hold values from -0.1875 to 0.1875
- couple_up: bfloat16 [8, 1024, 1024], P('freq', 'wall'), parts along dimension 0, may hold values from -0.03125 to 0.03125
- couple_down: bfloat16 [8, 1024, 1024], P('freq', 'wall'), parts along dimension 0, may hold values from -0.03125 to 0.03125
- strip_harmonics: int32 [8], P('freq'), parts along dimension 0, may hold values from 0 to 3
Outputs:
- basis: float32 [32, 1024, 128], P(('freq', 'harm'), 'wall'), parts along dimension 0
- triangle: float32 [256, 128], P('freq'), parts along dimension 0
There are 2 independent parts, one for each index of `freq`. A program takes and returns all parts, laid end to end along the dimension named above; each array names one. Nothing has to cross between parts.
Inputs may be any that keep to these rules, and one draw needn't show every extreme that they name: `strip_harmonics`: each entry one of 0 to 3; entries may repeat.
All inputs are finite; a program needn't handle non-finite values.
Results may differ from a plain program's by a relative error of at most 0.0045.
Values may be sent and summed in bfloat16 or wider, within the bound.
A program may use at most 64 MiB of HBM per device.

v0:
```python
import jax
import jax.numpy as jnp
from jax import lax
from jax.sharding import PartitionSpec as P

BAND = 4
SWEEPS = 3


def padded(cells, sides, width):
    for axis, dim in sides:
        count = lax.axis_size(axis)
        head = lax.slice_in_dim(cells, 0, width, axis=dim)
        tail = lax.slice_in_dim(cells, cells.shape[dim] - width, cells.shape[dim], axis=dim)
        cells = jnp.concatenate(
            [
                lax.ppermute(tail, axis, [(i, (i + 1) % count) for i in range(count)]),
                cells,
                lax.ppermute(head, axis, [((i + 1) % count, i) for i in range(count)]),
            ],
            axis=dim,
        )
    return cells


def body(sketch, inverse_blocks, couple_up, couple_down, strip_harmonics):
    offsets = strip_harmonics + 1
    local_count = sketch.shape[0]
    row_count = sketch.shape[1]
    width = sketch.shape[2]
    empty = jnp.zeros((local_count, row_count, width), jnp.float32)

    def add_inverse(piece):
        return jnp.einsum("hrc,hck->hrk", inverse_blocks, piece, preferred_element_type=jnp.float32)

    def apply_inverse(source):
        return add_inverse(lax.all_gather(source, "wall", axis=1, tiled=True))

    state = apply_inverse(sketch).astype(jnp.bfloat16)
    sampled = None
    for sweep in range(SWEEPS):
        extended = padded(state, (("harm", 0),), BAND)
        total = empty
        add_piece = lax.all_gather(extended, "wall", axis=1, tiled=True)
        for j in range(BAND):
            up_cols = couple_up[j]
            down_cols = couple_down[j]
            below = lax.dynamic_slice_in_dim(add_piece, BAND - offsets[j], local_count, 0)
            above = lax.dynamic_slice_in_dim(add_piece, BAND + offsets[j], local_count, 0)
            total = total + jnp.einsum(
                "rc,hck->hrk", up_cols, below, preferred_element_type=jnp.float32
            )
            total = total + jnp.einsum(
                "rc,hck->hrk", down_cols, above, preferred_element_type=jnp.float32
            )
        rhs = (sketch.astype(jnp.float32) - total).astype(jnp.bfloat16)
        result = apply_inverse(rhs)
        if sweep < SWEEPS - 1:
            state = result.astype(jnp.bfloat16)
        else:
            sampled = result
    flat = sampled.reshape(local_count * row_count, width)
    count = lax.axis_size("harm") * lax.axis_size("wall") * local_count * row_count
    local_gram = jnp.dot(
        flat.T, flat, precision=lax.Precision.HIGHEST, preferred_element_type=jnp.float32
    )
    gram = lax.psum(local_gram, ("harm", "wall")) / count
    lower = jnp.linalg.cholesky(gram)
    basis = jax.scipy.linalg.solve_triangular(lower, flat.T, lower=True).T
    triangle = lower.T
    return (basis.reshape(local_count, row_count, width), triangle)


def solution(mesh):
    return jax.shard_map(
        body,
        mesh=mesh,
        in_specs=(
            P(("freq", "harm"), "wall", None),
            P(("freq", "harm"), "wall", None),
            P("freq", "wall", None),
            P("freq", "wall", None),
            P("freq"),
        ),
        out_specs=(P(("freq", "harm"), "wall", None), P("freq", None)),
        check_vma=False,
    )
```

profile of v0, /device:TPU:8, one launch (start us, length us, event | category | flops | bytes accessed | tf_op | source)
XLA Modules:
  0.0 370.6 jit_solution(4480394632407928866)
XLA Ops:
  8.0 19.5 %all-gather.8.cloned.1.call-done = bf16[4,1024,128]{2,1,0:T(8,128)(2,1)} async-done(((bf16[4,256,128]{2,1,0:T(8,128)(2,1)}), bf16[4,1024,128]{2,1,0:T(8,128)(2,1)}) %all-gather.8.cloned.1.call-update) | async-done | bytes 1048592 | tf_op jit(solution)/shard_map/all_gather | solution.py:37
  27.4 1.9 convolution_convert_fusion.2
  31.5 6.4 %collective-permute-done.1 = bf16[4,256,128]{2,1,0:T(8,128)(2,1)S(1)} collective-permute-done((bf16[4,256,128]{2,1,0:T(8,128)(2,1)S(1)}, bf16[4,256,128]{2,1,0:T(8,128)(2,1)S(1)}, u32[]{:S(2)}, u32[]{:S(2)}) %collective-permute-start.1) | collective-permute-done | bytes 262176 | tf_op jit(solution)/shard_map/ppermute | solution.py:19
  37.9 7.5 %collective-permute-done = bf16[4,256,128]{2,1,0:T(8,128)(2,1)S(1)} collective-permute-done((bf16[4,256,128]{2,1,0:T(8,128)(2,1)S(1)}, bf16[4,256,128]{2,1,0:T(8,128)(2,1)S(1)}, u32[]{:S(2)}, u32[]{:S(2)}) %collective-permute-start) | collective-permute-done | bytes 262176 | tf_op jit(solution)/shard_map/ppermute | solution.py:17
  57.3 16.1 %all-gather.10.cloned.1.call-done = bf16[12,1024,128]{2,1,0:T(8,128)(2,1)} async-done(((bf16[12,256,128]{2,1,0:T(8,128)(2,1)}), bf16[12,1024,128]{2,1,0:T(8,128)(2,1)}) %all-gather.10.cloned.1.call-update) | async-done | bytes 3145744 | tf_op jit(solution)/shard_map/all_gather | solution.py:44
  73.4 2.0 fusion.35
  75.5 1.9 convolution_add_fusion.20
  77.3 1.7 convolution_add_fusion.19
  82.3 16.9 %all-gather.12.cloned.1.call-done = bf16[4,1024,128]{1,2,0:T(8,128)(2,1)} async-done(((bf16[4,256,128]{1,2,0:T(8,128)(2,1)}), bf16[4,1024,128]{1,2,0:T(8,128)(2,1)}) %all-gather.12.cloned.1.call-update) | async-done | bytes 1048592 | tf_op jit(solution)/shard_map/all_gather | solution.py:37
  99.3 2.1 fusion.9
  101.9 1.5 collective-permute-start.2
  103.4 6.4 %collective-permute-done.3 = bf16[4,256,128]{1,2,0:T(8,128)(2,1)S(1)} collective-permute-done((bf16[4,256,128]{1,2,0:T(8,128)(2,1)S(1)}, bf16[4,256,128]{1,2,0:T(8,128)(2,1)S(1)}, u32[]{:S(2)}, u32[]{:S(2)}) %collective-permute-start.3) | collective-permute-done | bytes 262176 | tf_op jit(solution)/shard_map/ppermute | solution.py:19
  109.8 7.5 %collective-permute-done.2 = bf16[4,256,128]{1,2,0:T(8,128)(2,1)S(1)} collective-permute-done((bf16[4,256,128]{1,2,0:T(8,128)(2,1)S(1)}, bf16[4,256,128]{1,2,0:T(8,128)(2,1)S(1)}, u32[]{:S(2)}, u32[]{:S(2)}) %collective-permute-start.2) | collective-permute-done | bytes 262176 | tf_op jit(solution)/shard_map/ppermute | solution.py:17
  118.4 27.4 %all-gather.14.cloned.1.call-done = bf16[12,1024,128]{1,2,0:T(8,128)(2,1)} async-done(((bf16[12,256,128]{1,2,0:T(8,128)(2,1)}), bf16[12,1024,128]{1,2,0:T(8,128)(2,1)}) %all-gather.14.cloned.1.call-update) | async-done | bytes 3145744 | tf_op jit(solution)/shard_map/all_gather | solution.py:44
  145.8 2.0 fusion.26
  147.8 1.8 convolution_add_fusion.13
  149.7 1.7 convolution_add_fusion.12
  154.6 16.9 %all-gather.16.cloned.1.call-done = bf16[4,1024,128]{1,2,0:T(8,128)(2,1)} async-done(((bf16[4,256,128]{1,2,0:T(8,128)(2,1)}), bf16[4,1024,128]{1,2,0:T(8,128)(2,1)}) %all-gather.16.cloned.1.call-update) | async-done | bytes 1048592 | tf_op jit(solution)/shard_map/all_gather | solution.py:37
  171.6 2.1 fusion.10
  174.2 1.5 collective-permute-start.4
  175.7 6.4 %collective-permute-done.5 = bf16[4,256,128]{1,2,0:T(8,128)(2,1)S(1)} collective-permute-done((bf16[4,256,128]{1,2,0:T(8,128)(2,1)S(1)}, bf16[4,256,128]{1,2,0:T(8,128)(2,1)S(1)}, u32[]{:S(2)}, u32[]{:S(2)}) %collective-permute-start.5) | collective-permute-done | bytes 262176 | tf_op jit(solution)/shard_map/ppermute | solution.py:19
  182.1 7.5 %collective-permute-done.4 = bf16[4,256,128]{1,2,0:T(8,128)(2,1)S(1)} collective-permute-done((bf16[4,256,128]{1,2,0:T(8,128)(2,1)S(1)}, bf16[4,256,128]{1,2,0:T(8,128)(2,1)S(1)}, u32[]{:S(2)}, u32[]{:S(2)}) %collective-permute-start.4) | collective-permute-done | bytes 262176 | tf_op jit(solution)/shard_map/ppermute | solution.py:17
  190.9 27.2 %all-gather.18.cloned.1.call-done = bf16[12,1024,128]{1,2,0:T(8,128)(2,1)} async-done(((bf16[12,256,128]{1,2,0:T(8,128)(2,1)}), bf16[12,1024,128]{1,2,0:T(8,128)(2,1)}) %all-gather.18.cloned.1.call-update) | async-done | bytes 3145744 | tf_op jit(solution)/shard_map/all_gather | solution.py:44
  218.1 2.0 fusion.17
  220.1 1.8 convolution_add_fusion.6
  222.0 1.7 convolution_add_fusion.5
  226.9 16.9 %all-gather.20.cloned.1.call-done = bf16[4,1024,128]{1,2,0:T(8,128)(2,1)} async-done(((bf16[4,256,128]{1,2,0:T(8,128)(2,1)}), bf16[4,1024,128]{1,2,0:T(8,128)(2,1)}) %all-gather.20.cloned.1.call-update) | async-done | bytes 1048592 | tf_op jit(solution)/shard_map/all_gather | solution.py:37
  243.9 2.1 convolution_bitcast_fusion
  247.2 89.4 %all-reduce.2.cloned.1.call-done = f32[128,128]{0,1:T(8,128)} async-done(((f32[128,128]{0,1:T(8,128)}), f32[128,128]{0,1:T(8,128)}) %all-reduce.2.cloned.1.call-update) | async-done | bytes 65552 | tf_op jit(solution)/shard_map/psum | solution.py:67
  338.4 11.7 %cholesky.16 = f32[128,128]{1,0:T(8,128)S(1)} custom-call(f32[128,128]{1,0:T(8,128)S(1)} %fusion.88), custom_call_target="Cholesky" | custom-call | tf_op jit(solution)/shard_map/jit(cholesky)/cholesky | solution.py:68
  352.2 9.8 %custom-call.7 = f32[1,128,128]{1,2,0:T(8,128)S(1)} custom-call(f32[1,128,128]{2,1,0:T(8,128)S(1)} %get-tuple-element.5), custom_call_target="InvertDiagBlocksLowerTriangular" | custom-call | tf_op jit(solution)/shard_map/jit(_solve_triangular)/triangular_solve | solution.py:69
  362.0 1.8 fusion.86
  (73 shorter events, 22.9 us)
Async XLA Ops:
  7.2 20.3 %copy-start = (bf16[4,256,1024]{2,1,0:T(8,128)(2,1)S(1)}, bf16[4,256,1024]{2,1,0:T(8,128)(2,1)}, u32[]{:S(2)}) copy-start(bf16[4,256,1024]{2,1,0:T(8,128)(2,1)} %param.6) | copy-start | bytes 6291460
  7.2 20.3 %all-gather.8.cloned.1.call-start = ((), (), s32[]{:S(2)}) async-start(), calls=%async_computation | async-start | bytes 1310720 | tf_op jit(solution)/shard_map/all_gather | solution.py:37
  7.9 65.5 %all-gather.10.cloned.1.call-start = ((), (), s32[]{:S(2)}) async-start(), calls=%async_computation.1 | async-start | bytes 3932160 | tf_op jit(solution)/shard_map/all_gather | solution.py:44
  29.4 17.1 %copy-start.11 = (s32[4]{0:T(128)S(1)}, s32[4]{0:T(128)}, u32[]{:S(2)}) copy-start(s32[4]{0:T(128)} %param.9) | copy-start | bytes 52
  29.4 27.7 %copy-start.10 = (bf16[4,256,128]{2,1,0:T(8,128)(2,1)S(1)}, bf16[4,256,128]{2,1,0:T(8,128)(2,1)}, u32[]{:S(2)}) copy-start(bf16[4,256,128]{2,1,0:T(8,128)(2,1)} %param.5) | copy-start | bytes 786436
  29.4 8.5 %collective-permute-start.1 = (bf16[4,256,128]{2,1,0:T(8,128)(2,1)S(1)}, bf16[4,256,128]{2,1,0:T(8,128)(2,1)S(1)}, u32[]{:S(2)}, u32[]{:S(2)}) collective-permute-start(bf16[4,256,128]{2,1,0:T(8,128)(2,1)S(1)} %convolution_convert_fusion.2), channel_id=1, source_target_pairs={{4,0},{8,4},{12,8},{0,12},{5,1},{9,5},{13,9},{1,13},{6,2},{10,6},{... | collective-permute-start | bytes 786440 | tf_op jit(solution)/shard_map/ppermute | solution.py:19
  30.0 15.4 %collective-permute-start = (bf16[4,256,128]{2,1,0:T(8,128)(2,1)S(1)}, bf16[4,256,128]{2,1,0:T(8,128)(2,1)S(1)}, u32[]{:S(2)}, u32[]{:S(2)}) collective-permute-start(bf16[4,256,128]{2,1,0:T(8,128)(2,1)S(1)} %convolution_convert_fusion.2), channel_id=1, source_target_pairs={{0,4},{4,8},{8,12},{12,0},{1,5},{5,9},{9,13},{13,1},{2,6},{6,10},{... | collective-permute-start | bytes 786440 | tf_op jit(solution)/shard_map/ppermute | solution.py:17
  46.4 52.9 %all-gather.12.cloned.1.call-start = ((), (), s32[]{:S(2)}) async-start(), calls=%async_computation.2 | async-start | bytes 1310720 | tf_op jit(solution)/shard_map/all_gather | solution.py:37
  73.4 2.1 copy-start.1
  75.5 3.6 copy-start.4
  75.5 3.6 copy-start.7
  82.3 63.5 %all-gather.14.cloned.1.call-start = ((), (), s32[]{:S(2)}) async-start(), calls=%async_computation.3 | async-start | bytes 3932160 | tf_op jit(solution)/shard_map/all_gather | solution.py:44
  101.3 8.5 %collective-permute-start.3 = (bf16[4,256,128]{1,2,0:T(8,128)(2,1)S(1)}, bf16[4,256,128]{1,2,0:T(8,128)(2,1)S(1)}, u32[]{:S(2)}, u32[]{:S(2)}) collective-permute-start(bf16[4,256,128]{1,2,0:T(8,128)(2,1)S(1)} %fusion.9), channel_id=1, source_target_pairs={{4,0},{8,4},{12,8},{0,12},{5,1},{9,5},{13,9},{1,13},{6,2},{10,6},{... | collective-permute-start | bytes 786440 | tf_op jit(solution)/shard_map/ppermute | solution.py:19
  101.9 15.4 %collective-permute-start.2 = (bf16[4,256,128]{1,2,0:T(8,128)(2,1)S(1)}, bf16[4,256,128]{1,2,0:T(8,128)(2,1)S(1)}, u32[]{:S(2)}, u32[]{:S(2)}) collective-permute-start(bf16[4,256,128]{1,2,0:T(8,128)(2,1)S(1)} %fusion.9), channel_id=1, source_target_pairs={{0,4},{4,8},{8,12},{12,0},{1,5},{5,9},{9,13},{13,1},{2,6},{6,10},{... | collective-permute-start | bytes 786440 | tf_op jit(solution)/shard_map/ppermute | solution.py:17
  118.3 53.2 %all-gather.16.cloned.1.call-start = ((), (), s32[]{:S(2)}) async-start(), calls=%async_computation.4 | async-start | bytes 1310720 | tf_op jit(solution)/shard_map/all_gather | solution.py:37
  145.8 2.1 copy-start.2
  147.8 3.6 copy-start.6
  147.8 3.6 copy-start.8
  154.6 63.5 %all-gather.18.cloned.1.call-start = ((), (), s32[]{:S(2)}) async-start(), calls=%async_computation.5 | async-start | bytes 3932160 | tf_op jit(solution)/shard_map/all_gather | solution.py:44
  173.6 8.5 %collective-permute-start.5 = (bf16[4,256,128]{1,2,0:T(8,128)(2,1)S(1)}, bf16[4,256,128]{1,2,0:T(8,128)(2,1)S(1)}, u32[]{:S(2)}, u32[]{:S(2)}) collective-permute-start(bf16[4,256,128]{1,2,0:T(8,128)(2,1)S(1)} %fusion.10), channel_id=1, source_target_pairs={{4,0},{8,4},{12,8},{0,12},{5,1},{9,5},{13,9},{1,13},{6,2},{10,6},{... | collective-permute-start | bytes 786440 | tf_op jit(solution)/shard_map/ppermute | solution.py:19
  174.2 15.4 %collective-permute-start.4 = (bf16[4,256,128]{1,2,0:T(8,128)(2,1)S(1)}, bf16[4,256,128]{1,2,0:T(8,128)(2,1)S(1)}, u32[]{:S(2)}, u32[]{:S(2)}) collective-permute-start(bf16[4,256,128]{1,2,0:T(8,128)(2,1)S(1)} %fusion.10), channel_id=1, source_target_pairs={{0,4},{4,8},{8,12},{12,0},{1,5},{5,9},{9,13},{13,1},{2,6},{6,10},{... | collective-permute-start | bytes 786440 | tf_op jit(solution)/shard_map/ppermute | solution.py:17
  190.6 53.2 %all-gather.20.cloned.1.call-start = ((), (), s32[]{:S(2)}) async-start(), calls=%async_computation.6 | async-start | bytes 1310720 | tf_op jit(solution)/shard_map/all_gather | solution.py:37
  218.1 2.1 copy-start.3
  220.1 3.6 copy-start.5
  220.1 3.6 copy-start.9
  226.9 109.7 %all-reduce.2.cloned.1.call-start = ((), (), s32[]{:S(2)}) async-start(), calls=%async_computation.7 | async-start | bytes 131072 | tf_op jit(solution)/shard_map/psum | solution.py:67
Sparse Core Ops, SparseCore 0:
  9.5 17.8 all-gather.7
  46.5 26.8 all-gather.9
  82.4 16.8 all-gather.11
  118.5 27.2 all-gather.13
  154.7 16.8 all-gather.15
  190.8 27.2 all-gather.17
  227.0 16.8 all-gather.19
  247.9 88.6 all-reduce.1
where the time goes:
time: 371 us
  waiting for transfers between devices  273 us (74%)
  matrix products  37.1 us (10%)
  other arithmetic  27.5 us (7%)
  between operations  24.5 us (7%)
  starting transfers between devices  6.74 us (2%)
    psum x1, waiting for transfers between devices, body(): gram = lax.psum(local_gram, ('harm', 'wall')) / count  89.4 us
    all_gather x3, waiting for transfers between devices, body(): add_piece = lax.all_gather(extended, 'wall', axis=1, tiled=True)  70.7 us
    all_gather x4, waiting for transfers between devices, apply_inverse(): return add_inverse(lax.all_gather(source, 'wall', axis=1, tiled=True))  70.3 us
    ppermute x3, waiting for transfers between devices, padded(): lax.ppermute(tail, axis, [(i, (i + 1) % count) for i in range(count)])  22.5 us
    ppermute x3, waiting for transfers between devices, padded(): lax.ppermute(head, axis, [((i + 1) % count, i) for i in range(count)])  19.3 us
    dot_general x12, matrix products, body(): jnp.einsum('rc,hck->hrk', up_cols, below, preferred_element_type=jnp.floa...  13.6 us
    dot_general x12, matrix products, body(): jnp.einsum('rc,hck->hrk', down_cols, above, preferred_element_type=jnp.fl...  12.4 us
    another operation x3, other arithmetic, body(): lower = jnp.linalg.cholesky(gram)  12.4 us
  transfers between devices with their start and end apart: 14, of which 14 were waited for; matrix products, arithmetic and copies ran while one was open for 0% of the time, Pallas kernels for 0%

commit v1 on v0

--- a/solution.py
+++ b/solution.py
@@ -5,6 +5,12 @@
 
 BAND = 4
 SWEEPS = 3
+
+
+def add_all(x, axis):
+    pieces = lax.all_gather(x, axis, axis=0, tiled=False)
+    total = pieces.sum(axis=0)
+    return total
 
 
 def padded(cells, sides, width):
@@ -64,7 +70,7 @@
     local_gram = jnp.dot(
         flat.T, flat, precision=lax.Precision.HIGHEST, preferred_element_type=jnp.float32
     )
-    gram = lax.psum(local_gram, ("harm", "wall")) / count
+    gram = add_all(local_gram, ("harm", "wall")) / count
     lower = jnp.linalg.cholesky(gram)
     basis = jax.scipy.linalg.solve_triangular(lower, flat.T, lower=True).T
     triangle = lower.T

time: 371 us -> 321 us (0.87)
  waiting for transfers between devices: 273 us -> 220 us
    psum x1 -> x0, waiting for transfers between devices: 89.4 us -> none  [body(): gram = lax.psum(local_gram, ('harm', 'wall')) / count]
    all_gather x0 -> x1, waiting for transfers between devices: none -> 37 us  [add_all(): pieces = lax.all_gather(x, axis, axis=0, tiled=False)]
where the time goes in v1:
time: 321 us; the launch traced here: 318 us
  waiting for transfers between devices  220 us (69%)
  matrix products  37.1 us (12%)
  other arithmetic  27.1 us (8%)
  between operations  24.5 us (8%)
  starting transfers between devices  6.74 us (2%)
    all_gather x3, waiting for transfers between devices, body(): add_piece = lax.all_gather(extended, 'wall', axis=1, tiled=True)  70.7 us
    all_gather x4, waiting for transfers between devices, apply_inverse(): return add_inverse(lax.all_gather(source, 'wall', axis=1, tiled=True))  70.3 us
    all_gather x1, waiting for transfers between devices, add_all(): pieces = lax.all_gather(x, axis, axis=0, tiled=False)  37 us
    ppermute x3, waiting for transfers between devices, padded(): lax.ppermute(tail, axis, [(i, (i + 1) % count) for i in range(count)])  22.5 us
    ppermute x3, waiting for transfers between devices, padded(): lax.ppermute(head, axis, [((i + 1) % count, i) for i in range(count)])  19.3 us
    dot_general x12, matrix products, body(): jnp.einsum('rc,hck->hrk', up_cols, below, preferred_element_type=jnp.floa...  13.6 us
    dot_general x12, matrix products, body(): jnp.einsum('rc,hck->hrk', down_cols, above, preferred_element_type=jnp.fl...  12.4 us
    another operation x3, other arithmetic, body(): lower = jnp.linalg.cholesky(gram)  12.4 us
  transfers between devices with their start and end apart: 14, of which 14 were waited for; matrix products, arithmetic and copies ran while one was open for 0% of the time, Pallas kernels for 0%

profile of v1, /device:TPU:8, one launch (start us, length us, event | category | flops | bytes accessed | tf_op | source)
XLA Modules:
  0.0 317.8 jit_solution(14829234867465790897)
XLA Ops:
  8.0 19.5 %all-gather.10.cloned.1.call-done = bf16[4,1024,128]{2,1,0:T(8,128)(2,1)} async-done(((bf16[4,256,128]{2,1,0:T(8,128)(2,1)}), bf16[4,1024,128]{2,1,0:T(8,128)(2,1)}) %all-gather.10.cloned.1.call-update) | async-done | bytes 1048592 | tf_op jit(solution)/shard_map/all_gather | solution.py:43
  27.4 1.9 convolution_convert_fusion.2
  31.5 6.4 %collective-permute-done.1 = bf16[4,256,128]{2,1,0:T(8,128)(2,1)S(1)} collective-permute-done((bf16[4,256,128]{2,1,0:T(8,128)(2,1)S(1)}, bf16[4,256,128]{2,1,0:T(8,128)(2,1)S(1)}, u32[]{:S(2)}, u32[]{:S(2)}) %collective-permute-start.1) | collective-permute-done | bytes 262176 | tf_op jit(solution)/shard_map/ppermute | solution.py:25
  37.9 7.5 %collective-permute-done = bf16[4,256,128]{2,1,0:T(8,128)(2,1)S(1)} collective-permute-done((bf16[4,256,128]{2,1,0:T(8,128)(2,1)S(1)}, bf16[4,256,128]{2,1,0:T(8,128)(2,1)S(1)}, u32[]{:S(2)}, u32[]{:S(2)}) %collective-permute-start) | collective-permute-done | bytes 262176 | tf_op jit(solution)/shard_map/ppermute | solution.py:23
  57.3 16.1 %all-gather.12.cloned.1.call-done = bf16[12,1024,128]{2,1,0:T(8,128)(2,1)} async-done(((bf16[12,256,128]{2,1,0:T(8,128)(2,1)}), bf16[12,1024,128]{2,1,0:T(8,128)(2,1)}) %all-gather.12.cloned.1.call-update) | async-done | bytes 3145744 | tf_op jit(solution)/shard_map/all_gather | solution.py:50
  73.4 2.0 fusion.35
  75.5 1.9 convolution_add_fusion.20
  77.3 1.7 convolution_add_fusion.19
  82.3 16.9 %all-gather.14.cloned.1.call-done = bf16[4,1024,128]{1,2,0:T(8,128)(2,1)} async-done(((bf16[4,256,128]{1,2,0:T(8,128)(2,1)}), bf16[4,1024,128]{1,2,0:T(8,128)(2,1)}) %all-gather.14.cloned.1.call-update) | async-done | bytes 1048592 | tf_op jit(solution)/shard_map/all_gather | solution.py:43
  99.3 2.1 fusion.9
  101.9 1.5 collective-permute-start.2
  103.4 6.4 %collective-permute-done.3 = bf16[4,256,128]{1,2,0:T(8,128)(2,1)S(1)} collective-permute-done((bf16[4,256,128]{1,2,0:T(8,128)(2,1)S(1)}, bf16[4,256,128]{1,2,0:T(8,128)(2,1)S(1)}, u32[]{:S(2)}, u32[]{:S(2)}) %collective-permute-start.3) | collective-permute-done | bytes 262176 | tf_op jit(solution)/shard_map/ppermute | solution.py:25
  109.8 7.5 %collective-permute-done.2 = bf16[4,256,128]{1,2,0:T(8,128)(2,1)S(1)} collective-permute-done((bf16[4,256,128]{1,2,0:T(8,128)(2,1)S(1)}, bf16[4,256,128]{1,2,0:T(8,128)(2,1)S(1)}, u32[]{:S(2)}, u32[]{:S(2)}) %collective-permute-start.2) | collective-permute-done | bytes 262176 | tf_op jit(solution)/shard_map/ppermute | solution.py:23
  118.4 27.4 %all-gather.16.cloned.1.call-done = bf16[12,1024,128]{1,2,0:T(8,128)(2,1)} async-done(((bf16[12,256,128]{1,2,0:T(8,128)(2,1)}), bf16[12,1024,128]{1,2,0:T(8,128)(2,1)}) %all-gather.16.cloned.1.call-update) | async-done | bytes 3145744 | tf_op jit(solution)/shard_map/all_gather | solution.py:50
  145.8 2.0 fusion.26
  147.8 1.8 convolution_add_fusion.13
  149.7 1.7 convolution_add_fusion.12
  154.6 16.9 %all-gather.18.cloned.1.call-done = bf16[4,1024,128]{1,2,0:T(8,128)(2,1)} async-done(((bf16[4,256,128]{1,2,0:T(8,128)(2,1)}), bf16[4,1024,128]{1,2,0:T(8,128)(2,1)}) %all-gather.18.cloned.1.call-update) | async-done | bytes 1048592 | tf_op jit(solution)/shard_map/all_gather | solution.py:43
  171.6 2.1 fusion.10
  174.2 1.5 collective-permute-start.4
  175.7 6.4 %collective-permute-done.5 = bf16[4,256,128]{1,2,0:T(8,128)(2,1)S(1)} collective-permute-done((bf16[4,256,128]{1,2,0:T(8,128)(2,1)S(1)}, bf16[4,256,128]{1,2,0:T(8,128)(2,1)S(1)}, u32[]{:S(2)}, u32[]{:S(2)}) %collective-permute-start.5) | collective-permute-done | bytes 262176 | tf_op jit(solution)/shard_map/ppermute | solution.py:25
  182.1 7.5 %collective-permute-done.4 = bf16[4,256,128]{1,2,0:T(8,128)(2,1)S(1)} collective-permute-done((bf16[4,256,128]{1,2,0:T(8,128)(2,1)S(1)}, bf16[4,256,128]{1,2,0:T(8,128)(2,1)S(1)}, u32[]{:S(2)}, u32[]{:S(2)}) %collective-permute-start.4) | collective-permute-done | bytes 262176 | tf_op jit(solution)/shard_map/ppermute | solution.py:23
  190.9 27.2 %all-gather.20.cloned.1.call-done = bf16[12,1024,128]{1,2,0:T(8,128)(2,1)} async-done(((bf16[12,256,128]{1,2,0:T(8,128)(2,1)}), bf16[12,1024,128]{1,2,0:T(8,128)(2,1)}) %all-gather.20.cloned.1.call-update) | async-done | bytes 3145744 | tf_op jit(solution)/shard_map/all_gather | solution.py:50
  218.1 2.0 fusion.17
  220.1 1.8 convolution_add_fusion.6
  222.0 1.7 convolution_add_fusion.5
  226.9 16.9 %all-gather.22.cloned.1.call-done = bf16[4,1024,128]{1,2,0:T(8,128)(2,1)} async-done(((bf16[4,256,128]{1,2,0:T(8,128)(2,1)}), bf16[4,1024,128]{1,2,0:T(8,128)(2,1)}) %all-gather.22.cloned.1.call-update) | async-done | bytes 1048592 | tf_op jit(solution)/shard_map/all_gather | solution.py:43
  243.9 2.1 convolution_bitcast_fusion
  247.2 37.0 %all-gather.24.cloned.1.call-done = f32[2048,128]{1,0:T(8,128)} async-done(((f32[128,128]{1,0:T(8,128)}), f32[2048,128]{1,0:T(8,128)}) %all-gather.24.cloned.1.call-update) | async-done | bytes 1048592 | tf_op jit(solution)/shard_map/all_gather | solution.py:11
  285.5 11.7 %cholesky.16 = f32[128,128]{1,0:T(8,128)S(1)} custom-call(f32[128,128]{1,0:T(8,128)S(1)} %fusion.88), custom_call_target="Cholesky" | custom-call | tf_op jit(solution)/shard_map/jit(cholesky)/cholesky | solution.py:74
  299.3 9.8 %custom-call.7 = f32[1,128,128]{1,2,0:T(8,128)S(1)} custom-call(f32[1,128,128]{2,1,0:T(8,128)S(1)} %get-tuple-element.7), custom_call_target="InvertDiagBlocksLowerTriangular" | custom-call | tf_op jit(solution)/shard_map/jit(_solve_triangular)/triangular_solve | solution.py:75
  309.1 1.8 fusion.86
  (73 shorter events, 22.5 us)
Async XLA Ops:
  7.2 20.3 %copy-start = (bf16[4,256,1024]{2,1,0:T(8,128)(2,1)S(1)}, bf16[4,256,1024]{2,1,0:T(8,128)(2,1)}, u32[]{:S(2)}) copy-start(bf16[4,256,1024]{2,1,0:T(8,128)(2,1)} %param.6) | copy-start | bytes 6291460
  7.2 20.3 %all-gather.10.cloned.1.call-start = ((), (), s32[]{:S(2)}) async-start(), calls=%async_computation | async-start | bytes 1310720 | tf_op jit(solution)/shard_map/all_gather | solution.py:43
  7.9 65.5 %all-gather.12.cloned.1.call-start = ((), (), s32[]{:S(2)}) async-start(), calls=%async_computation.1 | async-start | bytes 3932160 | tf_op jit(solution)/shard_map/all_gather | solution.py:50
  29.4 17.1 %copy-start.11 = (s32[4]{0:T(128)S(1)}, s32[4]{0:T(128)}, u32[]{:S(2)}) copy-start(s32[4]{0:T(128)} %param.9) | copy-start | bytes 52
  29.4 27.7 %copy-start.10 = (bf16[4,256,128]{2,1,0:T(8,128)(2,1)S(1)}, bf16[4,256,128]{2,1,0:T(8,128)(2,1)}, u32[]{:S(2)}) copy-start(bf16[4,256,128]{2,1,0:T(8,128)(2,1)} %param.5) | copy-start | bytes 786436
  29.4 8.5 %collective-permute-start.1 = (bf16[4,256,128]{2,1,0:T(8,128)(2,1)S(1)}, bf16[4,256,128]{2,1,0:T(8,128)(2,1)S(1)}, u32[]{:S(2)}, u32[]{:S(2)}) collective-permute-start(bf16[4,256,128]{2,1,0:T(8,128)(2,1)S(1)} %convolution_convert_fusion.2), channel_id=1, source_target_pairs={{4,0},{8,4},{12,8},{0,12},{5,1},{9,5},{13,9},{1,13},{6,2},{10,6},{... | collective-permute-start | bytes 786440 | tf_op jit(solution)/shard_map/ppermute | solution.py:25
  30.0 15.4 %collective-permute-start = (bf16[4,256,128]{2,1,0:T(8,128)(2,1)S(1)}, bf16[4,256,128]{2,1,0:T(8,128)(2,1)S(1)}, u32[]{:S(2)}, u32[]{:S(2)}) collective-permute-start(bf16[4,256,128]{2,1,0:T(8,128)(2,1)S(1)} %convolution_convert_fusion.2), channel_id=1, source_target_pairs={{0,4},{4,8},{8,12},{12,0},{1,5},{5,9},{9,13},{13,1},{2,6},{6,10},{... | collective-permute-start | bytes 786440 | tf_op jit(solution)/shard_map/ppermute | solution.py:23
  46.4 52.9 %all-gather.14.cloned.1.call-start = ((), (), s32[]{:S(2)}) async-start(), calls=%async_computation.2 | async-start | bytes 1310720 | tf_op jit(solution)/shard_map/all_gather | solution.py:43
  73.4 2.1 copy-start.1
  75.5 3.6 %copy-start.4 = (bf16[12,1024,128]{2,1,0:T(8,128)(2,1)S(1)}, bf16[12,1024,128]{2,1,0:T(8,128)(2,1)}, u32[]{:S(2)}) copy-start(bf16[12,1024,128]{2,1,0:T(8,128)(2,1)} %all-gather.12.cloned.1.call-done) | copy-start | bytes 9437188
  75.5 3.6 %copy-start.7 = (bf16[4,256,1024]{2,1,0:T(8,128)(2,1)S(1)}, bf16[4,256,1024]{2,1,0:T(8,128)(2,1)}, u32[]{:S(2)}) copy-start(bf16[4,256,1024]{2,1,0:T(8,128)(2,1)} %param.8) | copy-start | bytes 6291460
  82.3 63.5 %all-gather.16.cloned.1.call-start = ((), (), s32[]{:S(2)}) async-start(), calls=%async_computation.3 | async-start | bytes 3932160 | tf_op jit(solution)/shard_map/all_gather | solution.py:50
  101.3 8.5 %collective-permute-start.3 = (bf16[4,256,128]{1,2,0:T(8,128)(2,1)S(1)}, bf16[4,256,128]{1,2,0:T(8,128)(2,1)S(1)}, u32[]{:S(2)}, u32[]{:S(2)}) collective-permute-start(bf16[4,256,128]{1,2,0:T(8,128)(2,1)S(1)} %fusion.9), channel_id=1, source_target_pairs={{4,0},{8,4},{12,8},{0,12},{5,1},{9,5},{13,9},{1,13},{6,2},{10,6},{... | collective-permute-start | bytes 786440 | tf_op jit(solution)/shard_map/ppermute | solution.py:25
  101.9 15.4 %collective-permute-start.2 = (bf16[4,256,128]{1,2,0:T(8,128)(2,1)S(1)}, bf16[4,256,128]{1,2,0:T(8,128)(2,1)S(1)}, u32[]{:S(2)}, u32[]{:S(2)}) collective-permute-start(bf16[4,256,128]{1,2,0:T(8,128)(2,1)S(1)} %fusion.9), channel_id=1, source_target_pairs={{0,4},{4,8},{8,12},{12,0},{1,5},{5,9},{9,13},{13,1},{2,6},{6,10},{... | collective-permute-start | bytes 786440 | tf_op jit(solution)/shard_map/ppermute | solution.py:23
  118.3 53.2 %all-gather.18.cloned.1.call-start = ((), (), s32[]{:S(2)}) async-start(), calls=%async_computation.4 | async-start | bytes 1310720 | tf_op jit(solution)/shard_map/all_gather | solution.py:43
  145.8 2.1 copy-start.2
  147.8 3.6 %copy-start.6 = (bf16[12,1024,128]{1,2,0:T(8,128)(2,1)S(1)}, bf16[12,1024,128]{1,2,0:T(8,128)(2,1)}, u32[]{:S(2)}) copy-start(bf16[12,1024,128]{1,2,0:T(8,128)(2,1)} %all-gather.16.cloned.1.call-done) | copy-start | bytes 9437188
  147.8 3.6 %copy-start.8 = (bf16[4,256,1024]{2,1,0:T(8,128)(2,1)S(1)}, bf16[4,256,1024]{2,1,0:T(8,128)(2,1)}, u32[]{:S(2)}) copy-start(bf16[4,256,1024]{2,1,0:T(8,128)(2,1)} %param.8) | copy-start | bytes 6291460
  154.6 63.5 %all-gather.20.cloned.1.call-start = ((), (), s32[]{:S(2)}) async-start(), calls=%async_computation.5 | async-start | bytes 3932160 | tf_op jit(solution)/shard_map/all_gather | solution.py:50
  173.6 8.5 %collective-permute-start.5 = (bf16[4,256,128]{1,2,0:T(8,128)(2,1)S(1)}, bf16[4,256,128]{1,2,0:T(8,128)(2,1)S(1)}, u32[]{:S(2)}, u32[]{:S(2)}) collective-permute-start(bf16[4,256,128]{1,2,0:T(8,128)(2,1)S(1)} %fusion.10), channel_id=1, source_target_pairs={{4,0},{8,4},{12,8},{0,12},{5,1},{9,5},{13,9},{1,13},{6,2},{10,6},{... | collective-permute-start | bytes 786440 | tf_op jit(solution)/shard_map/ppermute | solution.py:25
  174.2 15.4 %collective-permute-start.4 = (bf16[4,256,128]{1,2,0:T(8,128)(2,1)S(1)}, bf16[4,256,128]{1,2,0:T(8,128)(2,1)S(1)}, u32[]{:S(2)}, u32[]{:S(2)}) collective-permute-start(bf16[4,256,128]{1,2,0:T(8,128)(2,1)S(1)} %fusion.10), channel_id=1, source_target_pairs={{0,4},{4,8},{8,12},{12,0},{1,5},{5,9},{9,13},{13,1},{2,6},{6,10},{... | collective-permute-start | bytes 786440 | tf_op jit(solution)/shard_map/ppermute | solution.py:23
  190.6 53.2 %all-gather.22.cloned.1.call-start = ((), (), s32[]{:S(2)}) async-start(), calls=%async_computation.6 | async-start | bytes 1310720 | tf_op jit(solution)/shard_map/all_gather | solution.py:43
  218.1 2.1 copy-start.3
  220.1 3.6 %copy-start.5 = (bf16[12,1024,128]{1,2,0:T(8,128)(2,1)S(1)}, bf16[12,1024,128]{1,2,0:T(8,128)(2,1)}, u32[]{:S(2)}) copy-start(bf16[12,1024,128]{1,2,0:T(8,128)(2,1)} %all-gather.20.cloned.1.call-done) | copy-start | bytes 9437188
  220.1 3.6 %copy-start.9 = (bf16[4,256,1024]{2,1,0:T(8,128)(2,1)S(1)}, bf16[4,256,1024]{2,1,0:T(8,128)(2,1)}, u32[]{:S(2)}) copy-start(bf16[4,256,1024]{2,1,0:T(8,128)(2,1)} %param.8) | copy-start | bytes 6291460
  226.9 57.3 %all-gather.24.cloned.1.call-start = ((), (), s32[]{:S(2)}) async-start(), calls=%async_computation.7 | async-start | bytes 1114112 | tf_op jit(solution)/shard_map/all_gather | solution.py:11
Sparse Core Ops, SparseCore 0:
  9.5 17.8 all-gather.9
  46.5 26.8 all-gather.11
  82.4 16.8 all-gather.13
  118.5 27.2 all-gather.15
  154.7 16.8 all-gather.17
  190.8 27.2 all-gather.19
  227.0 16.8 all-gather.21
  247.3 36.8 all-gather.23
